TPU v7x, 32 devices: a whole 2x2x4 slice. The times are simulated.
32 devices in a mesh: gx: 4 (over y, x), gy: 8 (over z, core).
Axes of the slice: x: 2, y: 2, z: 4, core: 2. Of those that a mesh axis runs over, the one named last changes fastest.
Arguments:
- thermal_field: float32 [192, 192, 128], P('gx', 'gy'), may hold values from -6 to 6
- generator_keys: int32 [6], replicated, may hold values from 0 to 1048575
- slab_top_offset: int32 [1], replicated, may hold values from 0 to 2047
Outputs:
- factor_x: float32 [192, 64], P('gx')
- factor_y: float32 [192, 64], P('gy')
- factor_z: float32 [128, 64], replicated
- core: float32 [128, 128, 128], P('gx', 'gy')
All inputs are finite; a program needn't handle non-finite values.
Results may differ from a plain program's by a relative error of at most 0.000071.
Values sent between devices are 32-bit elements; how exact they have to be, the bound alone decides.
A program may use at most 64 MiB of HBM per device.

v0:
```python
import math

import jax
import jax.numpy as jnp
from jax import lax
from jax.sharding import PartitionSpec as P

RANK = 64
TARGET_RANK = 128


def random_signs(seed_value, cell_index, column_index):
    hashed = cell_index * 73856093 + column_index * 19349663 + seed_value * 83492791
    hashed = jnp.bitwise_xor(hashed, lax.shift_right_logical(hashed, jnp.full_like(hashed, 15)))
    hashed = hashed * 668265261
    hashed = jnp.bitwise_xor(hashed, lax.shift_right_logical(hashed, jnp.full_like(hashed, 13)))
    parity = jnp.bitwise_and(
        lax.shift_right_logical(hashed, jnp.full_like(hashed, 7)), jnp.full_like(hashed, 1)
    )
    return jnp.where(parity == 1, 1.0, -1.0).astype(jnp.float32)


def body(thermal_field, generator_keys, slab_top_offset):
    exact_matmul_mode = lax.Precision.HIGHEST
    front_length, back_length, vertical_layer = thermal_field.shape
    devices_first = lax.axis_size("gx")
    devices_second = lax.axis_size("gy")
    total_first = front_length * devices_first
    total_second = back_length * devices_second
    x_index = (lax.axis_index("gx") * front_length + jnp.arange(front_length, dtype=jnp.int32))[
        :, None
    ]
    y_index = (lax.axis_index("gy") * back_length + jnp.arange(back_length, dtype=jnp.int32))[
        :, None
    ]
    z_index = (slab_top_offset[0] + jnp.arange(vertical_layer, dtype=jnp.int32))[:, None]
    rank_cols = jnp.arange(RANK, dtype=jnp.int32)[None, :]
    core_cols = jnp.arange(TARGET_RANK, dtype=jnp.int32)[None, :]
    omega_x = random_signs(generator_keys[0], x_index, rank_cols)
    omega_y = random_signs(generator_keys[1], y_index, rank_cols)
    omega_z = random_signs(generator_keys[2], z_index, rank_cols)
    phi_xt = random_signs(generator_keys[3], x_index, core_cols).T
    phi_yt = random_signs(generator_keys[4], y_index, core_cols).T
    phi_z = random_signs(generator_keys[5], z_index, core_cols)
    unrolled_grid = thermal_field.reshape(front_length * back_length, vertical_layer)
    reduced = jnp.dot(unrolled_grid, omega_z, precision=exact_matmul_mode).reshape(
        front_length, back_length, RANK
    )
    partial_x = jnp.einsum("xyk,yk->xk", reduced, omega_y, precision=exact_matmul_mode)
    partial_y = jnp.einsum("xyk,xk->yk", reduced, omega_x, precision=exact_matmul_mode)
    khatri = (omega_x[:, None, :] * omega_y[None, :, :]).reshape(front_length * back_length, RANK)
    partial_z = jnp.einsum("pz,pk->zk", unrolled_grid, khatri, precision=exact_matmul_mode)
    summed_x, half_z = lax.psum((partial_x, partial_z), "gy")
    summed_y, summed_z = lax.psum((partial_y, half_z), "gx")
    factor_x = summed_x * (1.0 / math.sqrt(total_second * vertical_layer))
    factor_y = summed_y * (1.0 / math.sqrt(total_first * vertical_layer))
    factor_z = summed_z * (1.0 / math.sqrt(total_first * total_second))
    thermal_matrix = thermal_field.reshape(front_length, back_length * vertical_layer)
    chosen_entries = phi_xt
    reduced_first = lax.psum_scatter(
        jnp.dot(chosen_entries, thermal_matrix, precision=exact_matmul_mode),
        "gx",
        scatter_dimension=0,
        tiled=True,
    )
    reduced_first = reduced_first.reshape(-1, back_length, vertical_layer)
    chosen_entries = phi_yt
    middle = jnp.einsum("by,ayz->baz", chosen_entries, reduced_first, precision=exact_matmul_mode)
    swapped = lax.psum_scatter(
        jnp.einsum("baz,zc->bac", middle, phi_z, precision=exact_matmul_mode),
        "gy",
        scatter_dimension=0,
        tiled=True,
    )
    core_block = jnp.transpose(swapped, (1, 0, 2))
    core = core_block * (1.0 / math.sqrt(total_first * total_second * vertical_layer))
    return (factor_x, factor_y, factor_z, core)


def solution(mesh):
    placed = (P("gx", "gy", None), P(), P())
    return jax.shard_map(
        body,
        mesh=mesh,
        in_specs=placed,
        out_specs=(P("gx", None), P("gy", None), P(), P("gx", "gy", None)),
        check_vma=False,
    )
```

profile of v0, /device:TPU:0, one launch (start us, length us, event | category | flops | bytes accessed | tf_op | source)
XLA Modules:
  0.0 114.7 jit_solution(7982089736002093003)
XLA Ops:
  7.2 0.0 reduce-scatter.3.cloned.1.call-start
  7.9 1.6 %fusion.115 = (s32[1]{0:T(128)}, s32[1]{0:T(128)}, s32[1]{0:T(128)}, s32[1]{0:T(128)}, s32[1]{0:T(128)}, /*index=5*/s32[1]{0:T(128)}) fusion(s32[6]{0:T(128)} %param.4), kind=kLoop, calls=%fused_computation.136 | loop fusion | bytes 48 | tf_op jit(solution)/shard_map/slice | solution.py:44
  10.1 3.7 %fusion = f32[128,3072]{1,0:T(8,128)} fusion(f32[6,8,24,128]{3,2,1,0:T(8,128)} %bitcast.47, s32[]{:T(128)} %bitcast.21, s32[128]{0:T(128)S(1)} %get-tuple-element.18, s32[48]{0:T(128)S(1)} %add_multiply_fusion), kind=kOutput, calls=%fused_computation.2 | convolution fusion | flops 226560000 | bytes 2163396 | tf_op jit(solution)/shard_map/dot_general | solution.py:61
  13.9 0.0 reduce-scatter.3.cloned.1.call-update
  13.9 0.0 reduce-scatter.5.cloned.1.call-start
  15.3 32.7 %reduce-scatter.3.cloned.1.call-done = f32[32,3072]{1,0:T(8,128)} async-done(((f32[128,3072]{1,0:T(8,128)}), f32[32,3072]{1,0:T(8,128)}) %reduce-scatter.3.cloned.1.call-update) | async-done | bytes 393232 | tf_op jit(solution)/shard_map/reduce_scatter | solution.py:60
  47.9 1.1 copy.27
  49.0 1.9 %fusion.60 = f32[128,32,128]{2,0,1:T(8,128)S(1)} fusion(f32[32,24,128]{2,1,0:T(8,128)S(1)} %bitcast.49, s32[]{:T(128)} %bitcast.19, s32[128]{0:T(128)S(1)} %get-tuple-element.18, s32[24]{0:T(128)S(1)} %add_multiply_fusion.2), kind=kOutput, calls=%fused_computation.75 | convolution fusion | flops 151028736 | bytes 2490980 | tf_op jit(solution)/shard_map/by,ayz->baz/dot_general | solution.py:68
  50.9 3.2 %fusion.15 = f32[128,32,128]{2,0,1:T(8,128)} fusion(f32[128,32,128]{2,0,1:T(8,128)S(1)} %fusion.60, s32[]{:T(128)} %bitcast.22, s32[128]{0:T(128)S(1)} %get-tuple-element.18, s32[128]{0:T(128)S(1)} %get-tuple-element.19), kind=kOutput, calls=%fused_computation.24 | convolution fusion | flops 805486592 | bytes 4195332 | tf_op jit(solution)/shard_map/baz,zc->bac/dot_general | solution.py:70
  54.1 0.0 copy-start
  54.2 0.0 reduce-scatter.5.cloned.1.call-update
  56.1 0.0 copy-done
  56.1 0.9 convolution_bitcast_fusion
  57.0 0.2 copy.22
  57.2 0.1 fusion.74
  57.3 0.1 multiply_reduce_fusion.1
  57.4 0.1 fusion.75
  57.5 1.2 %convolution_bitcast_fusion.1 = f32[128,64]{0,1:T(8,128)S(1)} fusion(f32[48,24,128]{2,1,0:T(8,128)S(1)} %copy-done, f32[24,64]{1,0:T(8,128)S(1)} %get-tuple-element.10, f32[48,64]{1,0:T(8,128)S(1)} %get-tuple-element.9), kind=kOutput, calls=%fused_computation.1 | convolution fusion | flops 113319936 | bytes 641024 | tf_op jit(solution)/shard_map/pz,pk->zk/dot_general | solution.py:52
  58.7 29.6 %all-reduce = (f32[48,64]{1,0:T(8,128)S(1)}, f32[128,64]{0,1:T(8,128)S(1)}) all-reduce(f32[48,64]{1,0:T(8,128)S(1)} %bitcast.51, f32[128,64]{0,1:T(8,128)S(1)} %convolution_bitcast_fusion.1), channel_id=1, replica_groups=mesh['gx'=4,'gy'=8] {'gy'}, use_global_device_ids=true, to_apply=%region_0.1 | all-reduce | flops 11264 | bytes 90112 | tf_op jit(solution)/shard_map/psum | solution.py:53
  88.2 0.1 multiply_reduce_fusion
  88.3 16.0 %all-reduce.1 = (f32[24,64]{1,0:T(8,128)S(1)}, f32[128,64]{0,1:T(8,128)S(1)}) all-reduce(f32[24,64]{1,0:T(8,128)S(1)} %bitcast.52, f32[128,64]{0,1:T(8,128)S(1)} %get-tuple-element.5), channel_id=1, replica_groups=mesh['gx'=4,'gy'=8] {'gx'}, use_global_device_ids=true, to_apply=%region_1.2 | all-reduce | flops 9728 | bytes 77824 | tf_op jit(solution)/shard_map/psum | solution.py:54
  104.3 0.6 broadcast_multiply_fusion.2
  105.0 0.6 broadcast_multiply_fusion.1
  105.6 0.6 broadcast_multiply_fusion
  106.2 0.0 reduce-scatter.5.cloned.1.call-done
  106.2 1.7 %multiply_bitcast_fusion = f32[32,16,128]{2,1,0:T(8,128)} fusion(f32[16,32,128]{2,0,1:T(8,128)} %reduce-scatter.5.cloned.1.call-done), kind=kLoop, calls=%fused_computation.11 | loop fusion | flops 65536 | bytes 524288 | tf_op jit(solution)/shard_map/mul | solution.py:76
  (4 shorter events, 0.0 us)
Async XLA Ops:
  7.2 40.8 %reduce-scatter.3.cloned.1.call-start = ((), (), s32[]{:S(2)}) async-start(), calls=%async_computation.2 | async-start | bytes 1966080 | tf_op jit(solution)/shard_map/reduce_scatter | solution.py:60
  13.9 92.3 %reduce-scatter.5.cloned.1.call-start = ((), (), s32[]{:S(2)}) async-start(), calls=%async_computation.3 | async-start | bytes 2359296 | tf_op jit(solution)/shard_map/reduce_scatter | solution.py:69
  54.1 2.0 %copy-start = (f32[48,24,128]{2,1,0:T(8,128)S(1)}, f32[48,24,128]{2,1,0:T(8,128)}, u32[]{:S(2)}) copy-start(f32[48,24,128]{2,1,0:T(8,128)} %param.3) | copy-start | bytes 1769476
Sparse Core Ops, SparseCore 0:
  14.0 33.8 reduce-scatter.2
  54.3 36.5 reduce-scatter.4
where the time goes:
time: 115 us
  blocking collectives  45.6 us (40%)
  waiting for transfers between devices  32.7 us (28%)
  between operations  18.7 us (16%)
  matrix products  10.9 us (9%)
  other arithmetic  3.9 us (3%)
  local copies, waits for them, and re-layouts  2.86 us (2%)
    reduce_scatter x1, waiting for transfers between devices, body(): lax.psum_scatter(jnp.dot(chosen_entries, thermal_matrix, precision=exact_...  32.7 us
    psum x1, blocking collectives, body(): summed_x, half_z = lax.psum((partial_x, partial_z), 'gy')  29.6 us
    psum x1, blocking collectives, body(): summed_y, summed_z = lax.psum((partial_y, half_z), 'gx')  16 us
    dot_general x1, matrix products, body(): jnp.dot(chosen_entries, thermal_matrix, precision=exact_matmul_mode)  3.73 us
    dot_general x1, matrix products, body(): jnp.einsum('baz,zc->bac', middle, phi_z, precision=exact_matmul_mode)  3.23 us
  transfers between devices with their start and end apart: 2, of which 1 were waited for; matrix products, arithmetic and copies ran while one was open for 4% of the time, Pallas kernels for 0%

commit v1 on v0

--- a/solution.py
+++ b/solution.py
@@ -1,8 +1,11 @@
+import functools
 import math
 
 import jax
 import jax.numpy as jnp
 from jax import lax
+from jax.experimental import pallas as pl
+from jax.experimental.pallas import tpu as pltpu
 from jax.sharding import PartitionSpec as P
 
 RANK = 64
@@ -77,10 +80,351 @@
     return (factor_x, factor_y, factor_z, core)
 
 
+SUB = 8
+LANES = 128
+MESH_ID = pl.DeviceIdType.MESH
+
+
+def signs(seed_value, cell_index, column_index):
+    hashed = cell_index * 73856093 + column_index * 19349663 + seed_value * 83492791
+    hashed = hashed ^ lax.shift_right_logical(hashed, jnp.full_like(hashed, 15))
+    hashed = hashed * 668265261
+    hashed = hashed ^ lax.shift_right_logical(hashed, jnp.full_like(hashed, 13))
+    return jnp.where((hashed & 128) != 0, 1.0, -1.0).astype(jnp.float32)
+
+
+def iota(shape, axis):
+    return lax.broadcasted_iota(jnp.int32, shape, axis)
+
+
+def split(value):
+    high = value.astype(jnp.bfloat16)
+    low = (value - high.astype(jnp.float32)).astype(jnp.bfloat16)
+    return high, low
+
+
+def mm(left, right):
+    return jnp.dot(left, right, preferred_element_type=jnp.float32)
+
+
+def flip(index, bit):
+    return index + bit - 2 * bit * ((index // bit) % 2)
+
+
+def kernel(
+    dims,
+    keys, top, field,
+    out_x, out_y, out_z, out_core,
+    spread, landed, own, near, far_out, far_in, done_out, done_in, kron,
+    small_out, small_in, small_sum, zsum_in, zx_out, zx_in, fy_out, fy_in,
+    s1, r1, s2, r2, s3, r3, s4, r4, t1, u1, t2, u2, t3, u3, t4, u4,
+):
+    nx, ng, front, back, depth = dims
+    nz = ng // 2
+    blk_a = TARGET_RANK // nx
+    chunks = blk_a // (2 * SUB)
+    blk_b = TARGET_RANK // nz
+    out_b = blk_b // 2
+    ix = lax.axis_index("gx")
+    ig = lax.axis_index("gy")
+    iz, core = ig // 2, ig % 2
+
+    def dev_x(d):
+        r = ix
+        for bit in (1, 2):
+            if d & bit:
+                r = flip(r, bit)
+        return r
+
+    def dev_g(d):
+        r = ig
+        for bit in (1, 2, 4):
+            if d & bit:
+                r = flip(r, bit)
+        return r
+
+    def copy(src, dst, send, recv, dx, dg):
+        return pltpu.make_async_remote_copy(
+            src_ref=src, dst_ref=dst, send_sem=send, recv_sem=recv,
+            device_id=(dev_x(dx), dev_g(dg)), device_id_type=MESH_ID,
+        )
+
+    partners = [(dx, dc) for dx in range(nx) for dc in range(2) if dx or dc]
+    partners += [(0, dg) for dg in range(2, ng)]
+    barrier = pltpu.get_barrier_semaphore()
+    for dx, dg in partners:
+        pl.semaphore_signal(
+            barrier, inc=1, device_id=(dev_x(dx), dev_g(dg)), device_id_type=MESH_ID
+        )
+
+    x0 = ix * front
+    y0 = ig * back
+    z0 = top[0]
+
+    rows = TARGET_RANK + RANK
+    row = iota((rows, 2 * front), 0)
+    lane = iota((rows, 2 * front), 1)
+    cell = jnp.where(lane >= front, lane - front, lane) + x0
+    is_core = row < TARGET_RANK
+    left = signs(
+        jnp.where(is_core, keys[3], keys[0]),
+        cell,
+        jnp.where(is_core, row, row - TARGET_RANK),
+    ).astype(jnp.bfloat16)
+    omega_yt = signs(keys[1], iota((RANK, back), 1) + y0, iota((RANK, back), 0))
+    total_z = jnp.zeros((RANK, depth), jnp.float32)
+    for y in range(back):
+        high, low = split(field[pl.ds(y, front, stride=back), :])
+        both = mm(left, jnp.concatenate([high, low], axis=0))
+        spread[y] = both[:TARGET_RANK]
+        total_z = total_z + both[TARGET_RANK:] * omega_yt[:, y : y + 1]
+
+    pl.semaphore_wait(barrier, len(partners))
+
+    pend = []
+    first = []
+    order = [d for d in ((3, 0), (3, 1), (1, 0), (2, 0), (1, 1), (2, 1), (0, 1))]
+    for i in range(chunks):
+        group = []
+        for dx, dc in order:
+            slot = dx * 2 + dc - 1
+            start = dev_x(dx) * blk_a + i * 2 * SUB + (dev_g(dc) % 2) * SUB
+            start = pl.multiple_of(start, SUB)
+            group.append(copy(
+                spread.at[:, pl.ds(start, SUB), :], landed.at[i, slot],
+                s1.at[i, slot], r1.at[i, slot], dx, dc,
+            ))
+            group[-1].start()
+        first.append(group)
+        pend += group
+
+    lane_z = iota((depth, LANES), 1)
+    row_z = iota((depth, LANES), 0) + z0
+    omega_z = signs(keys[2], row_z, lane_z).astype(jnp.bfloat16)
+    high, low = split(field[...])
+    reduced = (mm(high, omega_z) + mm(low, omega_z)).reshape(front, back, LANES)
+    omega_y = signs(keys[1], iota((back, LANES), 0) + y0, iota((back, LANES), 1))
+    part_y = jnp.zeros((back, LANES), jnp.float32)
+    omega_x = signs(keys[0], iota((front, LANES), 0) + x0, iota((front, LANES), 1))
+    part_x = jnp.sum(reduced * omega_y[None], axis=1)
+    for x in range(front):
+        part_y = part_y + reduced[x] * omega_x[x : x + 1]
+    fy_out[...] = part_y
+    per = front // ng
+    kper = RANK // ng
+    for d in range(ng):
+        small_out[d, 0:kper] = total_z[d * kper : (d + 1) * kper]
+        small_out[d, SUB : SUB + per] = part_x[d * per : (d + 1) * per]
+    fy = []
+    for d in range(1, nx):
+        fy.append(copy(fy_out, fy_in.at[d - 1], t1.at[d - 1], u1.at[d - 1], d, 0))
+        fy[-1].start()
+    sm = []
+    for d in range(1, ng):
+        sm.append(copy(
+            small_out.at[dev_g(d)], small_in.at[d - 1], t2.at[d - 1], u2.at[d - 1], 0, d
+        ))
+        sm[-1].start()
+    pend += fy
+
+    half = 2 * back * SUB
+    for dst in range(2):
+        for src in range(2):
+            for dc in range(2):
+                shape = (blk_b * SUB, back * SUB)
+                row = iota(shape, 0)
+                col = iota(shape, 1)
+                chip_b = (flip(iz, 2) if dst else iz) * blk_b
+                cell_y = dev_g(src * 2 + dc) * back
+                value = signs(
+                    keys[4],
+                    lax.shift_right_logical(col, jnp.full_like(col, 3)) + cell_y,
+                    lax.shift_right_logical(row, jnp.full_like(row, 3)) + chip_b,
+                )
+                value = jnp.where((row & 7) == (col & 7), value, 0.0)
+                kron[src, dc, dst * blk_b * SUB : (dst + 1) * blk_b * SUB, :] = value.astype(
+                    jnp.bfloat16
+                )
+    phi_z = signs(keys[5], row_z, lane_z).astype(jnp.bfloat16)
+
+    def project(src, dc, block):
+        high, low = split(block.reshape(back * SUB, depth))
+        return mm(kron[src, dc], high) + mm(kron[src, dc], low)
+
+    nearby = []
+    sums = []
+    for i in range(chunks):
+        for c in first[i]:
+            c.wait_recv()
+        for dc in range(2):
+            if dc:
+                base = landed[i, 0]
+            else:
+                base = spread[:, pl.ds(
+                    pl.multiple_of(ix * blk_a + i * 2 * SUB + core * SUB, SUB), SUB), :]
+            for dx in range(1, nx):
+                base = base + landed[i, dx * 2 + dc - 1]
+            own[i, dc] = base
+        c = copy(own.at[i], near.at[i], s2.at[i], r2.at[i], 0, 2)
+        c.start()
+        nearby.append(c)
+        sums.append(project(0, 0, own[i, 0]) + project(0, 1, own[i, 1]))
+    pend += nearby
+
+    for c in sm:
+        c.wait_recv()
+    block = small_out[ig]
+    for d in range(1, ng):
+        block = block + small_in[d - 1]
+    small_sum[...] = block
+    zx = []
+    for d in range(1, nx):
+        zx.append(copy(
+            small_sum.at[0:SUB], zsum_in.at[d - 1], t3.at[d - 1], u3.at[d - 1], d, 0
+        ))
+        zx[-1].start()
+    pend += zx
+
+    far = []
+    for i in range(chunks):
+        nearby[i].wait_recv()
+        total = sums[i] + project(1, 0, near[i, 0]) + project(1, 1, near[i, 1])
+        far_out[i] = total[blk_b * SUB :]
+        c = copy(far_out.at[i], far_in.at[i], s3.at[i], r3.at[i], 0, 4)
+        c.start()
+        far.append(c)
+        sums[i] = total[: blk_b * SUB]
+    pend += far
+
+    for c in zx:
+        c.wait_recv()
+    zpart = small_sum[0:SUB]
+    for d in range(1, nx):
+        zpart = zpart + zsum_in[d - 1]
+    zx_out[0:SUB] = zpart
+    zx_out[SUB:] = small_sum[SUB:]
+    gathered = []
+    for d in range(1, ng):
+        gathered.append(copy(zx_out, zx_in.at[d - 1], t4.at[d - 1], u4.at[d - 1], 0, d))
+        gathered[-1].start()
+    pend += gathered
+    for c in fy:
+        c.wait_recv()
+    value = fy_out[...]
+    for d in range(1, nx):
+        value = value + fy_in[d - 1]
+    out_y[...] = (value * (1.0 / math.sqrt(front * nx * depth)))[:, :RANK]
+
+    scale = 1.0 / math.sqrt(front * nx * back * ng * depth)
+    finals = []
+    for i in range(chunks):
+        far[i].wait_recv()
+        high, low = split(sums[i] + far_in[i])
+        value = (mm(high, phi_z) + mm(low, phi_z)) * scale
+        done_out[i] = value.reshape(2, out_b * SUB, depth)
+        c = copy(done_out.at[i, 1 - core], done_in.at[i], s4.at[i], r4.at[i], 0, 1)
+        c.start()
+        finals.append(c)
+        mine = done_out[i, core]
+        for b in range(out_b):
+            out_core[pl.ds((i * 2 * SUB + core * SUB) * out_b + b, SUB, stride=out_b), :] = (
+                mine[b * SUB : (b + 1) * SUB]
+            )
+    pend += finals
+
+    for c in gathered:
+        c.wait_recv()
+    for c in sm:
+        c.wait_send()
+    for d in range(ng):
+        block = zx_out[...] if d == 0 else zx_in[d - 1]
+        small_out[dev_g(d)] = block
+    scale_x = 1.0 / math.sqrt(back * ng * depth)
+    scale_z = 1.0 / math.sqrt(front * nx * back * ng)
+    for d in range(ng):
+        out_x[d * per : (d + 1) * per, :] = small_out[d, SUB : SUB + per, :RANK] * scale_x
+    whole = jnp.concatenate([small_out[d, 0:kper] for d in range(ng)], axis=0)
+    out_z[...] = whole.T * scale_z
+
+    for i in range(chunks):
+        finals[i].wait_recv()
+        other = done_in[i]
+        for b in range(out_b):
+            out_core[
+                pl.ds((i * 2 * SUB + (1 - core) * SUB) * out_b + b, SUB, stride=out_b), :
+            ] = other[b * SUB : (b + 1) * SUB]
+    for c in pend:
+        c.wait_send()
+
+
+def fused_body(nx, ng, thermal_field, generator_keys, slab_top_offset):
+    front, back, depth = thermal_field.shape
+    nz = ng // 2
+    blk_a = TARGET_RANK // nx
+    chunks = blk_a // (2 * SUB)
+    blk_b = TARGET_RANK // nz
+    out_b = blk_b // 2
+    f32 = jnp.float32
+    vmem = pltpu.VMEM
+    dma = pltpu.SemaphoreType.DMA
+    peers = 2 * nx - 1
+    scratch = [
+        vmem((back, TARGET_RANK, depth), f32),
+        vmem((chunks, peers, back, SUB, depth), f32),
+        vmem((chunks, 2, back, SUB, depth), f32),
+        vmem((chunks, 2, back, SUB, depth), f32),
+        vmem((chunks, blk_b * SUB, depth), f32),
+        vmem((chunks, blk_b * SUB, depth), f32),
+        vmem((chunks, 2, out_b * SUB, depth), f32),
+        vmem((chunks, out_b * SUB, depth), f32),
+        vmem((2, 2, 2 * blk_b * SUB, back * SUB), jnp.bfloat16),
+        vmem((ng, 2 * SUB, LANES), f32),
+        vmem((ng - 1, 2 * SUB, LANES), f32),
+        vmem((2 * SUB, LANES), f32),
+        vmem((nx - 1, SUB, LANES), f32),
+        vmem((2 * SUB, LANES), f32),
+        vmem((ng - 1, 2 * SUB, LANES), f32),
+        vmem((back, LANES), f32),
+        vmem((nx - 1, back, LANES), f32),
+        dma((chunks, peers)), dma((chunks, peers)),
+        dma((chunks,)), dma((chunks,)),
+        dma((chunks,)), dma((chunks,)),
+        dma((chunks,)), dma((chunks,)),
+        dma((nx - 1,)), dma((nx - 1,)),
+        dma((ng - 1,)), dma((ng - 1,)),
+        dma((nx - 1,)), dma((nx - 1,)),
+        dma((ng - 1,)), dma((ng - 1,)),
+    ]
+    whole = pl.BlockSpec(memory_space=pltpu.VMEM)
+    scalar = pl.BlockSpec(memory_space=pltpu.SMEM)
+    fx, fy, fz, core = pl.pallas_call(
+        functools.partial(kernel, (nx, ng, front, back, depth)),
+        out_shape=(
+            jax.ShapeDtypeStruct((front, RANK), f32),
+            jax.ShapeDtypeStruct((back, RANK), f32),
+            jax.ShapeDtypeStruct((depth, RANK), f32),
+            jax.ShapeDtypeStruct((blk_a * out_b, depth), f32),
+        ),
+        in_specs=[scalar, scalar, whole],
+        out_specs=(whole,) * 4,
+        scratch_shapes=scratch,
+        compiler_params=pltpu.CompilerParams(
+            collective_id=0, has_side_effects=True, vmem_limit_bytes=40 * 2**20
+        ),
+    )(generator_keys, slab_top_offset, thermal_field.reshape(front * back, depth))
+    return fx, fy, fz, core.reshape(blk_a, out_b, depth)
+
+
+def suits(nx, ng):
+    return nx == 4 and ng == 8
+
+
 def solution(mesh):
+    nx, ng = mesh.shape["gx"], mesh.shape["gy"]
+    chosen = functools.partial(fused_body, nx, ng) if suits(nx, ng) else body
     placed = (P("gx", "gy", None), P(), P())
     return jax.shard_map(
-        body,
+        chosen,
         mesh=mesh,
         in_specs=placed,
         out_specs=(P("gx", None), P("gy", None), P(), P("gx", "gy", None)),

time: 115 us -> 49 us (0.43)
  blocking collectives: 45.6 us -> 0 us
  Pallas kernels: 0 us -> 43.2 us
  waiting for transfers between devices: 32.7 us -> 0 us
  between operations: 18.7 us -> 1.3 us
  matrix products: 10.9 us -> 0 us
  other arithmetic: 3.9 us -> 0 us
  local copies, waits for them, and re-layouts: 2.86 us -> 4.32 us
    psum x2 -> x0, blocking collectives: 45.6 us -> none  [the longest x1 29.6 us: body(): summed_x, half_z = lax.psum((partial_x, partial_z), 'gy')]
    pallas_call x0 -> x1, Pallas kernels: none -> 43.2 us  [fused_body(): pl.pallas_call(functools.partial(kernel, (nx, ng, front, back, depth)), o...]
    reduce_scatter x2 -> x0, waiting for transfers between devices: 32.7 us -> none  [the longest x1 32.7 us: body(): lax.psum_scatter(jnp.dot(chosen_entries, thermal_matrix, precision=exact_...]
    dot_general x5 -> x0, matrix products: 10.9 us -> none  [the longest x1 3.73 us: body(): jnp.dot(chosen_entries, thermal_matrix, precision=exact_matmul_mode)]
    mul x8 -> x0, other arithmetic: 3.53 us -> none  [the longest x1 1.68 us: body(): core_block * (1.0 / math.sqrt(total_first * total_second * vertical_layer))]
    unnamed x4 -> x8, local copies, waits for them, and re-layouts: 1.3 us -> 4.32 us
    slice x1 -> x0, local copies, waits for them, and re-layouts: 1.56 us -> none  [body(): phi_z = random_signs(generator_keys[5], z_index, core_cols)]
  transfers between devices with their start and end apart: 2 -> 0, of which waited for: 1 -> 0; matrix products, arithmetic and copies ran while one was open for 4% -> 0% of each run, Pallas kernels for 0% -> 0%
where the time goes in v1:
time: 49 us; the launch traced here: 48.9 us
  Pallas kernels  43.2 us (88%)
  local copies, waits for them, and re-layouts  4.32 us (9%)
  between operations  1.3 us (3%)
    pallas_call x1, Pallas kernels, fused_body(): pl.pallas_call(functools.partial(kernel, (nx, ng, front, back, depth)), o...  43.2 us
    unnamed x8, local copies, waits for them, and re-layouts  4.32 us

profile of v1, /device:TPU:0, one launch (start us, length us, event | category | flops | bytes accessed | tf_op | source)
XLA Modules:
  0.0 48.9 jit_solution(67693153929799964)
XLA Ops:
  1.3 0.0 copy-start.1
  1.3 0.6 %copy-done.1 = s32[6]{0:T(128)S(1)} copy-done((s32[6]{0:T(128)S(1)}, s32[6]{0:T(128)}, u32[]{:S(2)}) %copy-start.1) | copy-done | bytes 48
  1.9 0.0 copy-start
  1.9 1.1 %copy-done = f32[48,24,128]{2,1,0:T(8,128)S(1)} copy-done((f32[48,24,128]{2,1,0:T(8,128)S(1)}, f32[48,24,128]{2,1,0:T(8,128)}, u32[]{:S(2)}) %copy-start) | copy-done | bytes 589848
  3.0 43.2 %shard_map.66 = (f32[48,64]{1,0:T(8,128)S(1)}, f32[24,64]{1,0:T(8,128)S(1)}, f32[128,64]{1,0:T(8,128)S(1)}, f32[512,128]{1,0:T(8,128)S(1)}) custom-call(s32[6]{0:T(128)S(1)} %copy-done.1, s32[1]{0:T(128)S(6)} %copy.11.top, f32[1152,128]{1,0:T(8,128)S(1)} %bitcast.2), custom_call_target="tpu_custom_call" | custom-call | tf_op jit(solution)/shard_map/pallas_call | solution.py:400
  46.3 0.7 %copy.7 = f32[128,64]{0,1:T(8,128)} copy(f32[128,64]{1,0:T(8,128)S(1)} %get-tuple-element.14) | data formatting | bytes 65536
  47.0 0.6 %copy.12 = f32[48,64]{1,0:T(8,128)} copy(f32[48,64]{1,0:T(8,128)S(1)} %get-tuple-element.20) | data formatting | bytes 24576
  47.6 0.6 %copy.13 = f32[24,64]{1,0:T(8,128)} copy(f32[24,64]{1,0:T(8,128)S(1)} %get-tuple-element.21) | data formatting | bytes 12288
  48.2 0.7 %copy.14 = f32[32,16,128]{2,1,0:T(8,128)} copy(f32[32,16,128]{2,1,0:T(8,128)S(1)} %bitcast.3) | data formatting | bytes 524288
Async XLA Ops:
  1.3 0.7 %copy-start.1 = (s32[6]{0:T(128)S(1)}, s32[6]{0:T(128)}, u32[]{:S(2)}) copy-start(s32[6]{0:T(128)} %keys.1) | copy-start | bytes 76
  1.9 1.1 %copy-start = (f32[48,24,128]{2,1,0:T(8,128)S(1)}, f32[48,24,128]{2,1,0:T(8,128)}, u32[]{:S(2)}) copy-start(f32[48,24,128]{2,1,0:T(8,128)} %param.3) | copy-start | bytes 1769476

commit v2 on v1

--- a/solution.py
+++ b/solution.py
@@ -111,13 +111,26 @@
     return index + bit - 2 * bit * ((index // bit) % 2)
 
 
+def way_of(group, groups, core):
+    if 2 * group + 1 == groups:
+        return core
+    return 0 if 2 * group < groups else 1
+
+
+def step_x(ix, way, turn):
+    low = flip(ix, 1)
+    high = flip(ix, 2)
+    first = low + (high - low) * way
+    return first if turn == 0 else low + high - first
+
+
 def kernel(
     dims,
     keys, top, field,
     out_x, out_y, out_z, out_core,
-    spread, landed, own, near, far_out, far_in, done_out, done_in, kron,
+    raw_in, spread, landed, own, near, far_out, far_in, done_out, done_in, kron,
     small_out, small_in, small_sum, zsum_in, zx_out, zx_in, fy_out, fy_in,
-    s1, r1, s2, r2, s3, r3, s4, r4, t1, u1, t2, u2, t3, u3, t4, u4,
+    s0, r0, s5, r5, s1, r1, s2, r2, s3, r3, s4, r4, t1, u1, t2, u2, t3, u3, t4, u4,
 ):
     nx, ng, front, back, depth = dims
     nz = ng // 2
@@ -161,47 +174,50 @@
     y0 = ig * back
     z0 = top[0]
 
-    rows = TARGET_RANK + RANK
-    row = iota((rows, 2 * front), 0)
-    lane = iota((rows, 2 * front), 1)
-    cell = jnp.where(lane >= front, lane - front, lane) + x0
-    is_core = row < TARGET_RANK
-    left = signs(
-        jnp.where(is_core, keys[3], keys[0]),
-        cell,
-        jnp.where(is_core, row, row - TARGET_RANK),
-    ).astype(jnp.bfloat16)
+    groups = back // SUB
+    two_d = field.reshape(front * back, depth)
+
+    pl.semaphore_wait(barrier, len(partners))
+    raws = []
+    for g in range(groups):
+        way = way_of(g, groups, core)
+        near_x = step_x(ix, way, 0)
+        raws.append(pltpu.make_async_remote_copy(
+            src_ref=field.at[:, g * SUB : (g + 1) * SUB, :], dst_ref=raw_in.at[g],
+            send_sem=s0.at[g], recv_sem=r0.at[g],
+            device_id=(near_x, ig), device_id_type=MESH_ID,
+        ))
+        raws[-1].start()
+    pend = list(raws)
+
+    x0 = ix * front
+    y0 = ig * back
+    z0 = top[0]
+    rows = 2 * blk_a + RANK
     omega_yt = signs(keys[1], iota((RANK, back), 1) + y0, iota((RANK, back), 0))
     total_z = jnp.zeros((RANK, depth), jnp.float32)
-    for y in range(back):
-        high, low = split(field[pl.ds(y, front, stride=back), :])
-        both = mm(left, jnp.concatenate([high, low], axis=0))
-        spread[y] = both[:TARGET_RANK]
-        total_z = total_z + both[TARGET_RANK:] * omega_yt[:, y : y + 1]
-
-    pl.semaphore_wait(barrier, len(partners))
-
-    pend = []
-    first = []
-    order = [d for d in ((3, 0), (3, 1), (1, 0), (2, 0), (1, 1), (2, 1), (0, 1))]
-    for i in range(chunks):
-        group = []
-        for dx, dc in order:
-            slot = dx * 2 + dc - 1
-            start = dev_x(dx) * blk_a + i * 2 * SUB + (dev_g(dc) % 2) * SUB
-            start = pl.multiple_of(start, SUB)
-            group.append(copy(
-                spread.at[:, pl.ds(start, SUB), :], landed.at[i, slot],
-                s1.at[i, slot], r1.at[i, slot], dx, dc,
-            ))
-            group[-1].start()
-        first.append(group)
-        pend += group
+    for g in range(groups):
+        way = way_of(g, groups, core)
+        row = iota((rows, 2 * front), 0)
+        lane = iota((rows, 2 * front), 1)
+        cell = jnp.where(lane >= front, lane - front, lane) + x0
+        target = jnp.where(row < blk_a, ix * blk_a, step_x(ix, way, 1) * blk_a - blk_a) + row
+        is_core = row < 2 * blk_a
+        left = signs(
+            jnp.where(is_core, keys[3], keys[0]),
+            cell,
+            jnp.where(is_core, target, row - 2 * blk_a),
+        ).astype(jnp.bfloat16)
+        for y in range(g * SUB, (g + 1) * SUB):
+            high, low = split(two_d[pl.ds(y, front, stride=back), :])
+            both = mm(left, jnp.concatenate([high, low], axis=0))
+            spread[y] = both[: 2 * blk_a]
+            total_z = total_z + both[2 * blk_a :] * omega_yt[:, y : y + 1]
 
     lane_z = iota((depth, LANES), 1)
     row_z = iota((depth, LANES), 0) + z0
     omega_z = signs(keys[2], row_z, lane_z).astype(jnp.bfloat16)
-    high, low = split(field[...])
+    high, low = split(two_d[...])
     reduced = (mm(high, omega_z) + mm(low, omega_z)).reshape(front, back, LANES)
     omega_y = signs(keys[1], iota((back, LANES), 0) + y0, iota((back, LANES), 1))
     part_y = jnp.zeros((back, LANES), jnp.float32)
@@ -251,20 +267,57 @@
         high, low = split(block.reshape(back * SUB, depth))
         return mm(kron[src, dc], high) + mm(kron[src, dc], low)
 
+    sends = [[] for _ in range(chunks)]
+
+    def send_far(i, g):
+        way = way_of(g, groups, core)
+        for dc in (1, 0):
+            start = blk_a + i * 2 * SUB + (dev_g(dc) % 2) * SUB
+            sends[i].append(pltpu.make_async_remote_copy(
+                src_ref=spread.at[g * SUB : (g + 1) * SUB, pl.ds(pl.multiple_of(start, SUB), SUB), :],
+                dst_ref=landed.at[i, dc, g * SUB : (g + 1) * SUB],
+                send_sem=s1.at[i, dc, g], recv_sem=r1.at[i, dc, g],
+                device_id=(step_x(ix, way, 1), dev_g(dc)), device_id_type=MESH_ID,
+            ))
+            sends[i][-1].start()
+
+    def send_core(i):
+        start = pl.multiple_of(i * 2 * SUB + (1 - core) * SUB, SUB)
+        sends[i].append(copy(
+            spread.at[:, pl.ds(start, SUB), :], landed.at[i, 2],
+            s5.at[i], r5.at[i], 0, 1,
+        ))
+        sends[i][-1].start()
+
+    for g in range(groups):
+        way = way_of(g, groups, core)
+        shape = (2 * blk_a, 2 * front)
+        row = iota(shape, 0)
+        lane = iota(shape, 1)
+        cell = jnp.where(lane >= front, lane - front, lane) + step_x(ix, way, 0) * front
+        target = jnp.where(row < blk_a, ix * blk_a, step_x(ix, way, 1) * blk_a - blk_a) + row
+        left = signs(keys[3], cell, target).astype(jnp.bfloat16)
+        raws[g].wait_recv()
+        flat = raw_in.at[g].reshape(front * SUB, depth)
+        for y in range(SUB):
+            high, low = split(flat[pl.ds(y, front, stride=SUB), :])
+            spread[g * SUB + y] += mm(left, jnp.concatenate([high, low], axis=0))
+        send_far(0, g)
+    send_core(0)
+    for i in range(1, chunks):
+        for g in range(groups):
+            send_far(i, g)
+        send_core(i)
+    pend += sum(sends, [])
+
     nearby = []
     sums = []
     for i in range(chunks):
-        for c in first[i]:
+        for c in sends[i]:
             c.wait_recv()
-        for dc in range(2):
-            if dc:
-                base = landed[i, 0]
-            else:
-                base = spread[:, pl.ds(
-                    pl.multiple_of(ix * blk_a + i * 2 * SUB + core * SUB, SUB), SUB), :]
-            for dx in range(1, nx):
-                base = base + landed[i, dx * 2 + dc - 1]
-            own[i, dc] = base
+        start = pl.multiple_of(i * 2 * SUB + core * SUB, SUB)
+        own[i, 0] = spread[:, pl.ds(start, SUB), :] + landed[i, 0]
+        own[i, 1] = landed[i, 2] + landed[i, 1]
         c = copy(own.at[i], near.at[i], s2.at[i], r2.at[i], 0, 2)
         c.start()
         nearby.append(c)
@@ -367,10 +420,11 @@
     f32 = jnp.float32
     vmem = pltpu.VMEM
     dma = pltpu.SemaphoreType.DMA
-    peers = 2 * nx - 1
+    groups = back // SUB
     scratch = [
-        vmem((back, TARGET_RANK, depth), f32),
-        vmem((chunks, peers, back, SUB, depth), f32),
+        vmem((groups, front, SUB, depth), f32),
+        vmem((back, 2 * blk_a, depth), f32),
+        vmem((chunks, 3, back, SUB, depth), f32),
         vmem((chunks, 2, back, SUB, depth), f32),
         vmem((chunks, 2, back, SUB, depth), f32),
         vmem((chunks, blk_b * SUB, depth), f32),
@@ -386,7 +440,9 @@
         vmem((ng - 1, 2 * SUB, LANES), f32),
         vmem((back, LANES), f32),
         vmem((nx - 1, back, LANES), f32),
-        dma((chunks, peers)), dma((chunks, peers)),
+        dma((groups,)), dma((groups,)),
+        dma((chunks,)), dma((chunks,)),
+        dma((chunks, 2, groups)), dma((chunks, 2, groups)),
         dma((chunks,)), dma((chunks,)),
         dma((chunks,)), dma((chunks,)),
         dma((chunks,)), dma((chunks,)),
@@ -411,7 +467,7 @@
         compiler_params=pltpu.CompilerParams(
             collective_id=0, has_side_effects=True, vmem_limit_bytes=40 * 2**20
         ),
-    )(generator_keys, slab_top_offset, thermal_field.reshape(front * back, depth))
+    )(generator_keys, slab_top_offset, thermal_field)
     return fx, fy, fz, core.reshape(blk_a, out_b, depth)
 
 

time: 49 us -> 47.3 us (0.965)
  Pallas kernels: 43.2 us -> 42.1 us
  local copies, waits for them, and re-layouts: 4.32 us -> 3.67 us
    pallas_call x1, Pallas kernels: 43.2 us -> 42.1 us  [fused_body(): pl.pallas_call(functools.partial(kernel, (nx, ng, front, back, depth)), o...]
    unnamed x8, local copies, waits for them, and re-layouts: 4.32 us -> 3.67 us
where the time goes in v2:
time: 47.3 us; the launch traced here: 47.1 us
  Pallas kernels  42.1 us (89%)
  local copies, waits for them, and re-layouts  3.67 us (8%)
  between operations  1.32 us (3%)
    pallas_call x1, Pallas kernels, fused_body(): pl.pallas_call(functools.partial(kernel, (nx, ng, front, back, depth)), o...  42.1 us
    unnamed x8, local copies, waits for them, and re-layouts  3.67 us

profile of v2, /device:TPU:0, one launch (start us, length us, event | category | flops | bytes accessed | tf_op | source)
XLA Modules:
  0.0 47.1 jit_solution(12800154145300433057)
XLA Ops:
  0.6 0.0 copy-start.1
  1.3 0.0 copy-done.1
  1.3 0.0 copy-start
  1.3 1.1 %copy-done = f32[48,24,128]{2,1,0:T(8,128)S(1)} copy-done((f32[48,24,128]{2,1,0:T(8,128)S(1)}, f32[48,24,128]{2,1,0:T(8,128)}, u32[]{:S(2)}) %copy-start) | copy-done | bytes 589848
  2.4 42.1 %shard_map.66 = (f32[48,64]{1,0:T(8,128)S(1)}, f32[24,64]{1,0:T(8,128)S(1)}, f32[128,64]{1,0:T(8,128)S(1)}, f32[512,128]{1,0:T(8,128)S(1)}) custom-call(s32[6]{0:T(128)S(1)} %copy-done.1, s32[1]{0:T(128)S(6)} %copy.11.top, f32[48,24,128]{2,1,0:T(8,128)S(1)} %copy-done), custom_call_target="tpu_custom_call" | custom-call | tf_op jit(solution)/shard_map/pallas_call | solution.py:456
  44.5 0.7 %copy.7 = f32[128,64]{0,1:T(8,128)} copy(f32[128,64]{1,0:T(8,128)S(1)} %get-tuple-element.14) | data formatting | bytes 65536
  45.2 0.6 %copy.12 = f32[48,64]{1,0:T(8,128)} copy(f32[48,64]{1,0:T(8,128)S(1)} %get-tuple-element.20) | data formatting | bytes 24576
  45.8 0.6 %copy.13 = f32[24,64]{1,0:T(8,128)} copy(f32[24,64]{1,0:T(8,128)S(1)} %get-tuple-element.21) | data formatting | bytes 12288
  46.4 0.7 %copy.14 = f32[32,16,128]{2,1,0:T(8,128)} copy(f32[32,16,128]{2,1,0:T(8,128)S(1)} %bitcast.1) | data formatting | bytes 524288
Async XLA Ops:
  0.6 0.7 %copy-start.1 = (s32[6]{0:T(128)S(1)}, s32[6]{0:T(128)}, u32[]{:S(2)}) copy-start(s32[6]{0:T(128)} %keys.1) | copy-start | bytes 76
  1.3 1.1 %copy-start = (f32[48,24,128]{2,1,0:T(8,128)S(1)}, f32[48,24,128]{2,1,0:T(8,128)}, u32[]{:S(2)}) copy-start(f32[48,24,128]{2,1,0:T(8,128)} %field.1) | copy-start | bytes 1769476

commit v3 on v2

--- a/solution.py
+++ b/solution.py
@@ -126,9 +126,9 @@
 
 def kernel(
     dims,
-    keys, top, field,
+    keys, top, field_in,
     out_x, out_y, out_z, out_core,
-    raw_in, spread, landed, own, near, far_out, far_in, done_out, done_in, kron,
+    field, load_sem, raw_out, raw_in, spread, landed, own, near, far_out, far_in, done_out, done_in, kron,
     small_out, small_in, small_sum, zsum_in, zx_out, zx_in, fy_out, fy_in,
     s0, r0, s5, r5, s1, r1, s2, r2, s3, r3, s4, r4, t1, u1, t2, u2, t3, u3, t4, u4,
 ):
@@ -175,44 +175,77 @@
     z0 = top[0]
 
     groups = back // SUB
+    fold = front // 2
+    deep = depth // 2
+    load = pltpu.make_async_copy(field_in, field, load_sem)
+    load.start()
     two_d = field.reshape(front * back, depth)
-
-    pl.semaphore_wait(barrier, len(partners))
-    raws = []
-    for g in range(groups):
-        way = way_of(g, groups, core)
-        near_x = step_x(ix, way, 0)
-        raws.append(pltpu.make_async_remote_copy(
-            src_ref=field.at[:, g * SUB : (g + 1) * SUB, :], dst_ref=raw_in.at[g],
-            send_sem=s0.at[g], recv_sem=r0.at[g],
-            device_id=(near_x, ig), device_id_type=MESH_ID,
-        ))
-        raws[-1].start()
-    pend = list(raws)
-
     x0 = ix * front
     y0 = ig * back
     z0 = top[0]
-    rows = 2 * blk_a + RANK
+    lower = iota((fold, SUB, depth), 2) < deep
+    raws = []
+    load.wait()
+    for h in range(2):
+        for g in range(groups):
+            here = field[0:fold, g * SUB : (g + 1) * SUB, :]
+            there = field[fold:front, g * SUB : (g + 1) * SUB, :]
+            if h == 0:
+                raw_out[h, g] = jnp.where(lower, here, pltpu.roll(there, deep, 2))
+            else:
+                raw_out[h, g] = jnp.where(lower, pltpu.roll(here, deep, 2), there)
+    pl.semaphore_wait(barrier, len(partners))
+    for h in range(2):
+        for g in range(groups):
+            near_x = step_x(ix, way_of(g, groups, core), 0)
+            raws.append(pltpu.make_async_remote_copy(
+                src_ref=raw_out.at[h, g], dst_ref=raw_in.at[h, g],
+                send_sem=s0.at[h, g], recv_sem=r0.at[h, g],
+                device_id=(near_x, ig), device_id_type=MESH_ID,
+            ))
+            raws[-1].start()
+    pend = list(raws)
+
+    pairs = blk_a // 2
+
+    def weights(base, far_x):
+        shape = (4 * pairs, 4 * fold)
+        row = iota(shape, 0)
+        lane = iota(shape, 1)
+        lane = jnp.where(lane >= front, lane - front, lane)
+        second = row >= 2 * pairs
+        row = jnp.where(second, row - 2 * pairs, row)
+        swapped = jnp.where(lane >= fold, lane - fold, lane + fold)
+        cell = jnp.where(second, swapped, lane) + base
+        target = jnp.where(row < pairs, ix * blk_a, far_x * blk_a - pairs) + row
+        target = jnp.where(second, target + pairs, target)
+        return signs(keys[3], cell, target).astype(jnp.bfloat16)
+
+    lower_row = iota((2 * pairs, depth), 1) < deep
+
+    def contract(left, packed):
+        both = jnp.concatenate([packed, pltpu.roll(packed, deep, 1)], axis=0)
+        high, low = split(both)
+        out = mm(left, jnp.concatenate([high, low], axis=0))
+        return jnp.where(lower_row, out[: 2 * pairs], out[2 * pairs :])
+
+    for g in range(groups):
+        way = way_of(g, groups, core)
+        left = weights(x0, step_x(ix, way, 1))
+        for h in range(2):
+            flat = raw_out.at[h, g].reshape(fold * SUB, depth)
+            for y in range(SUB):
+                spread[h, g * SUB + y] = contract(left, flat[pl.ds(y, fold, stride=SUB), :])
+    lane = iota((RANK, 2 * front), 1)
+    left = signs(
+        keys[0], jnp.where(lane >= front, lane - front, lane) + x0, iota((RANK, 2 * front), 0)
+    ).astype(jnp.bfloat16)
     omega_yt = signs(keys[1], iota((RANK, back), 1) + y0, iota((RANK, back), 0))
     total_z = jnp.zeros((RANK, depth), jnp.float32)
-    for g in range(groups):
-        way = way_of(g, groups, core)
-        row = iota((rows, 2 * front), 0)
-        lane = iota((rows, 2 * front), 1)
-        cell = jnp.where(lane >= front, lane - front, lane) + x0
-        target = jnp.where(row < blk_a, ix * blk_a, step_x(ix, way, 1) * blk_a - blk_a) + row
-        is_core = row < 2 * blk_a
-        left = signs(
-            jnp.where(is_core, keys[3], keys[0]),
-            cell,
-            jnp.where(is_core, target, row - 2 * blk_a),
-        ).astype(jnp.bfloat16)
-        for y in range(g * SUB, (g + 1) * SUB):
-            high, low = split(two_d[pl.ds(y, front, stride=back), :])
-            both = mm(left, jnp.concatenate([high, low], axis=0))
-            spread[y] = both[: 2 * blk_a]
-            total_z = total_z + both[2 * blk_a :] * omega_yt[:, y : y + 1]
+    for y in range(back):
+        high, low = split(two_d[pl.ds(y, front, stride=back), :])
+        both = mm(left, jnp.concatenate([high, low], axis=0))
+        total_z = total_z + both * omega_yt[:, y : y + 1]
 
     lane_z = iota((depth, LANES), 1)
     row_z = iota((depth, LANES), 0) + z0
@@ -261,53 +294,48 @@
                 kron[src, dc, dst * blk_b * SUB : (dst + 1) * blk_b * SUB, :] = value.astype(
                     jnp.bfloat16
                 )
-    phi_z = signs(keys[5], row_z, lane_z).astype(jnp.bfloat16)
+    row = iota((depth, 2 * LANES), 0)
+    col = iota((depth, 2 * LANES), 1)
+    same = (row >= deep) == (col >= LANES)
+    row = jnp.where(row >= deep, row - deep, row) + z0
+    col = jnp.where(col >= LANES, col - LANES, col)
+    phi_z = [
+        jnp.where(same, signs(keys[5], row + h * deep, col), 0.0).astype(jnp.bfloat16)
+        for h in range(2)
+    ]
 
     def project(src, dc, block):
         high, low = split(block.reshape(back * SUB, depth))
         return mm(kron[src, dc], high) + mm(kron[src, dc], low)
 
     sends = [[] for _ in range(chunks)]
-
-    def send_far(i, g):
+    lefts = []
+    for g in range(groups):
         way = way_of(g, groups, core)
-        for dc in (1, 0):
-            start = blk_a + i * 2 * SUB + (dev_g(dc) % 2) * SUB
-            sends[i].append(pltpu.make_async_remote_copy(
-                src_ref=spread.at[g * SUB : (g + 1) * SUB, pl.ds(pl.multiple_of(start, SUB), SUB), :],
-                dst_ref=landed.at[i, dc, g * SUB : (g + 1) * SUB],
-                send_sem=s1.at[i, dc, g], recv_sem=r1.at[i, dc, g],
-                device_id=(step_x(ix, way, 1), dev_g(dc)), device_id_type=MESH_ID,
-            ))
-            sends[i][-1].start()
-
-    def send_core(i):
-        start = pl.multiple_of(i * 2 * SUB + (1 - core) * SUB, SUB)
+        lefts.append(weights(step_x(ix, way, 0) * front, step_x(ix, way, 1)))
+    for i in range(chunks):
+        for g in range(groups):
+            raws[i * groups + g].wait_recv()
+            flat = raw_in.at[i, g].reshape(fold * SUB, depth)
+            for y in range(SUB):
+                spread[i, g * SUB + y] += contract(
+                    lefts[g], flat[pl.ds(y, fold, stride=SUB), :]
+                )
+            for dc in (1, 0):
+                start = pl.multiple_of(pairs + (dev_g(dc) % 2) * SUB, SUB)
+                sends[i].append(pltpu.make_async_remote_copy(
+                    src_ref=spread.at[i, g * SUB : (g + 1) * SUB, pl.ds(start, SUB), :],
+                    dst_ref=landed.at[i, dc, g * SUB : (g + 1) * SUB],
+                    send_sem=s1.at[i, dc, g], recv_sem=r1.at[i, dc, g],
+                    device_id=(step_x(ix, way_of(g, groups, core), 1), dev_g(dc)),
+                    device_id_type=MESH_ID,
+                ))
+                sends[i][-1].start()
+        start = pl.multiple_of((1 - core) * SUB, SUB)
         sends[i].append(copy(
-            spread.at[:, pl.ds(start, SUB), :], landed.at[i, 2],
-            s5.at[i], r5.at[i], 0, 1,
+            spread.at[i, :, pl.ds(start, SUB), :], landed.at[i, 2], s5.at[i], r5.at[i], 0, 1
         ))
         sends[i][-1].start()
-
-    for g in range(groups):
-        way = way_of(g, groups, core)
-        shape = (2 * blk_a, 2 * front)
-        row = iota(shape, 0)
-        lane = iota(shape, 1)
-        cell = jnp.where(lane >= front, lane - front, lane) + step_x(ix, way, 0) * front
-        target = jnp.where(row < blk_a, ix * blk_a, step_x(ix, way, 1) * blk_a - blk_a) + row
-        left = signs(keys[3], cell, target).astype(jnp.bfloat16)
-        raws[g].wait_recv()
-        flat = raw_in.at[g].reshape(front * SUB, depth)
-        for y in range(SUB):
-            high, low = split(flat[pl.ds(y, front, stride=SUB), :])
-            spread[g * SUB + y] += mm(left, jnp.concatenate([high, low], axis=0))
-        send_far(0, g)
-    send_core(0)
-    for i in range(1, chunks):
-        for g in range(groups):
-            send_far(i, g)
-        send_core(i)
     pend += sum(sends, [])
 
     nearby = []
@@ -315,8 +343,7 @@
     for i in range(chunks):
         for c in sends[i]:
             c.wait_recv()
-        start = pl.multiple_of(i * 2 * SUB + core * SUB, SUB)
-        own[i, 0] = spread[:, pl.ds(start, SUB), :] + landed[i, 0]
+        own[i, 0] = spread[i, :, pl.ds(pl.multiple_of(core * SUB, SUB), SUB), :] + landed[i, 0]
         own[i, 1] = landed[i, 2] + landed[i, 1]
         c = copy(own.at[i], near.at[i], s2.at[i], r2.at[i], 0, 2)
         c.start()
@@ -370,19 +397,28 @@
 
     scale = 1.0 / math.sqrt(front * nx * back * ng * depth)
     finals = []
+    mine = 0.0
+
+    def last(i, block):
+        high, low = split(block)
+        return mm(high, phi_z[i]) + mm(low, phi_z[i])
+
+    def put(which, value):
+        value = value * scale
+        for i in range(chunks):
+            for b in range(out_b):
+                out_core[pl.ds((i * pairs + which * SUB) * out_b + b, SUB, stride=out_b), :] = (
+                    value[b * SUB : (b + 1) * SUB, i * LANES : (i + 1) * LANES]
+                )
+
     for i in range(chunks):
         far[i].wait_recv()
-        high, low = split(sums[i] + far_in[i])
-        value = (mm(high, phi_z) + mm(low, phi_z)) * scale
-        done_out[i] = value.reshape(2, out_b * SUB, depth)
+        done_out[i] = (sums[i] + far_in[i]).reshape(2, out_b * SUB, depth)
         c = copy(done_out.at[i, 1 - core], done_in.at[i], s4.at[i], r4.at[i], 0, 1)
         c.start()
         finals.append(c)
-        mine = done_out[i, core]
-        for b in range(out_b):
-            out_core[pl.ds((i * 2 * SUB + core * SUB) * out_b + b, SUB, stride=out_b), :] = (
-                mine[b * SUB : (b + 1) * SUB]
-            )
+        mine = mine + last(i, done_out[i, core])
+    put(core, mine)
     pend += finals
 
     for c in gathered:
@@ -399,13 +435,11 @@
     whole = jnp.concatenate([small_out[d, 0:kper] for d in range(ng)], axis=0)
     out_z[...] = whole.T * scale_z
 
+    other = 0.0
     for i in range(chunks):
         finals[i].wait_recv()
-        other = done_in[i]
-        for b in range(out_b):
-            out_core[
-                pl.ds((i * 2 * SUB + (1 - core) * SUB) * out_b + b, SUB, stride=out_b), :
-            ] = other[b * SUB : (b + 1) * SUB]
+        other = other + last(i, done_in[i])
+    put(1 - core, other)
     for c in pend:
         c.wait_send()
 
@@ -422,8 +456,11 @@
     dma = pltpu.SemaphoreType.DMA
     groups = back // SUB
     scratch = [
-        vmem((groups, front, SUB, depth), f32),
-        vmem((back, 2 * blk_a, depth), f32),
+        vmem((front, back, depth), f32),
+        dma(()),
+        vmem((2, groups, front // 2, SUB, depth), f32),
+        vmem((2, groups, front // 2, SUB, depth), f32),
+        vmem((2, back, blk_a, depth), f32),
         vmem((chunks, 3, back, SUB, depth), f32),
         vmem((chunks, 2, back, SUB, depth), f32),
         vmem((chunks, 2, back, SUB, depth), f32),
@@ -440,7 +477,7 @@
         vmem((ng - 1, 2 * SUB, LANES), f32),
         vmem((back, LANES), f32),
         vmem((nx - 1, back, LANES), f32),
-        dma((groups,)), dma((groups,)),
+        dma((2, groups)), dma((2, groups)),
         dma((chunks,)), dma((chunks,)),
         dma((chunks, 2, groups)), dma((chunks, 2, groups)),
         dma((chunks,)), dma((chunks,)),
@@ -461,7 +498,7 @@
             jax.ShapeDtypeStruct((depth, RANK), f32),
             jax.ShapeDtypeStruct((blk_a * out_b, depth), f32),
         ),
-        in_specs=[scalar, scalar, whole],
+        in_specs=[scalar, scalar, pl.BlockSpec(memory_space=pl.ANY)],
         out_specs=(whole,) * 4,
         scratch_shapes=scratch,
         compiler_params=pltpu.CompilerParams(

time: 47.3 us -> 46 us (0.973)
  Pallas kernels: 42.1 us -> 40.7 us
    pallas_call x1, Pallas kernels: 42.1 us -> 40.7 us  [fused_body(): pl.pallas_call(functools.partial(kernel, (nx, ng, front, back, depth)), o...]
where the time goes in v3:
time: 46 us; the launch traced here: 45.7 us
  Pallas kernels  40.7 us (88%)
  local copies, waits for them, and re-layouts  3.67 us (8%)
  between operations  1.32 us (3%)
    pallas_call x1, Pallas kernels, fused_body(): pl.pallas_call(functools.partial(kernel, (nx, ng, front, back, depth)), o...  40.7 us
    unnamed x8, local copies, waits for them, and re-layouts  3.67 us

profile of v3, /device:TPU:0, one launch (start us, length us, event | category | flops | bytes accessed | tf_op | source)
XLA Modules:
  0.0 45.7 jit_solution(14077026156877280327)
XLA Ops:
  0.6 0.0 copy-start.1
  1.3 0.0 copy-done.1
  1.3 0.0 copy-start
  1.3 1.1 %copy-done = f32[48,24,128]{2,1,0:T(8,128)S(1)} copy-done((f32[48,24,128]{2,1,0:T(8,128)S(1)}, f32[48,24,128]{2,1,0:T(8,128)}, u32[]{:S(2)}) %copy-start) | copy-done | bytes 589848
  2.4 40.7 %shard_map.66 = (f32[48,64]{1,0:T(8,128)S(1)}, f32[24,64]{1,0:T(8,128)S(1)}, f32[128,64]{1,0:T(8,128)S(1)}, f32[512,128]{1,0:T(8,128)S(1)}) custom-call(s32[6]{0:T(128)S(1)} %copy-done.1, s32[1]{0:T(128)S(6)} %copy.11.top, f32[48,24,128]{2,1,0:T(8,128)S(1)} %copy-done), custom_call_target="tpu_custom_call" | custom-call | tf_op jit(solution)/shard_map/pallas_call | solution.py:493
  43.1 0.7 %copy.7 = f32[128,64]{0,1:T(8,128)} copy(f32[128,64]{1,0:T(8,128)S(1)} %get-tuple-element.14) | data formatting | bytes 65536
  43.8 0.6 %copy.12 = f32[48,64]{1,0:T(8,128)} copy(f32[48,64]{1,0:T(8,128)S(1)} %get-tuple-element.20) | data formatting | bytes 24576
  44.4 0.6 %copy.13 = f32[24,64]{1,0:T(8,128)} copy(f32[24,64]{1,0:T(8,128)S(1)} %get-tuple-element.21) | data formatting | bytes 12288
  45.0 0.7 %copy.14 = f32[32,16,128]{2,1,0:T(8,128)} copy(f32[32,16,128]{2,1,0:T(8,128)S(1)} %bitcast.1) | data formatting | bytes 524288
Async XLA Ops:
  0.6 0.7 %copy-start.1 = (s32[6]{0:T(128)S(1)}, s32[6]{0:T(128)}, u32[]{:S(2)}) copy-start(s32[6]{0:T(128)} %keys.1) | copy-start | bytes 76
  1.3 1.1 %copy-start = (f32[48,24,128]{2,1,0:T(8,128)S(1)}, f32[48,24,128]{2,1,0:T(8,128)}, u32[]{:S(2)}) copy-start(f32[48,24,128]{2,1,0:T(8,128)} %field_in.1) | copy-start | bytes 1769476

commit v4 on v3

--- a/solution.py
+++ b/solution.py
@@ -229,13 +229,42 @@
         out = mm(left, jnp.concatenate([high, low], axis=0))
         return jnp.where(lower_row, out[: 2 * pairs], out[2 * pairs :])
 
+    sends = [[] for _ in range(chunks)]
+    lefts = []
+    owns = []
     for g in range(groups):
         way = way_of(g, groups, core)
-        left = weights(x0, step_x(ix, way, 1))
-        for h in range(2):
-            flat = raw_out.at[h, g].reshape(fold * SUB, depth)
+        owns.append(weights(x0, step_x(ix, way, 1)))
+        lefts.append(weights(step_x(ix, way, 0) * front, step_x(ix, way, 1)))
+    for i in range(chunks):
+        for g in range(groups):
+            flat = raw_out.at[i, g].reshape(fold * SUB, depth)
             for y in range(SUB):
-                spread[h, g * SUB + y] = contract(left, flat[pl.ds(y, fold, stride=SUB), :])
+                spread[i, g * SUB + y] = contract(owns[g], flat[pl.ds(y, fold, stride=SUB), :])
+        for g in range(groups):
+            raws[i * groups + g].wait_recv()
+            flat = raw_in.at[i, g].reshape(fold * SUB, depth)
+            for y in range(SUB):
+                spread[i, g * SUB + y] += contract(
+                    lefts[g], flat[pl.ds(y, fold, stride=SUB), :]
+                )
+            for dc in (1, 0):
+                start = pl.multiple_of(pairs + (dev_g(dc) % 2) * SUB, SUB)
+                sends[i].append(pltpu.make_async_remote_copy(
+                    src_ref=spread.at[i, g * SUB : (g + 1) * SUB, pl.ds(start, SUB), :],
+                    dst_ref=landed.at[i, dc, g * SUB : (g + 1) * SUB],
+                    send_sem=s1.at[i, dc, g], recv_sem=r1.at[i, dc, g],
+                    device_id=(step_x(ix, way_of(g, groups, core), 1), dev_g(dc)),
+                    device_id_type=MESH_ID,
+                ))
+                sends[i][-1].start()
+        start = pl.multiple_of((1 - core) * SUB, SUB)
+        sends[i].append(copy(
+            spread.at[i, :, pl.ds(start, SUB), :], landed.at[i, 2], s5.at[i], r5.at[i], 0, 1
+        ))
+        sends[i][-1].start()
+    pend += sum(sends, [])
+
     lane = iota((RANK, 2 * front), 1)
     left = signs(
         keys[0], jnp.where(lane >= front, lane - front, lane) + x0, iota((RANK, 2 * front), 0)
@@ -307,36 +336,6 @@
     def project(src, dc, block):
         high, low = split(block.reshape(back * SUB, depth))
         return mm(kron[src, dc], high) + mm(kron[src, dc], low)
-
-    sends = [[] for _ in range(chunks)]
-    lefts = []
-    for g in range(groups):
-        way = way_of(g, groups, core)
-        lefts.append(weights(step_x(ix, way, 0) * front, step_x(ix, way, 1)))
-    for i in range(chunks):
-        for g in range(groups):
-            raws[i * groups + g].wait_recv()
-            flat = raw_in.at[i, g].reshape(fold * SUB, depth)
-            for y in range(SUB):
-                spread[i, g * SUB + y] += contract(
-                    lefts[g], flat[pl.ds(y, fold, stride=SUB), :]
-                )
-            for dc in (1, 0):
-                start = pl.multiple_of(pairs + (dev_g(dc) % 2) * SUB, SUB)
-                sends[i].append(pltpu.make_async_remote_copy(
-                    src_ref=spread.at[i, g * SUB : (g + 1) * SUB, pl.ds(start, SUB), :],
-                    dst_ref=landed.at[i, dc, g * SUB : (g + 1) * SUB],
-                    send_sem=s1.at[i, dc, g], recv_sem=r1.at[i, dc, g],
-                    device_id=(step_x(ix, way_of(g, groups, core), 1), dev_g(dc)),
-                    device_id_type=MESH_ID,
-                ))
-                sends[i][-1].start()
-        start = pl.multiple_of((1 - core) * SUB, SUB)
-        sends[i].append(copy(
-            spread.at[i, :, pl.ds(start, SUB), :], landed.at[i, 2], s5.at[i], r5.at[i], 0, 1
-        ))
-        sends[i][-1].start()
-    pend += sum(sends, [])
 
     nearby = []
     sums = []

time: 46 us -> 46.7 us (1.015)
  Pallas kernels: 40.7 us -> 41.4 us
    pallas_call x1, Pallas kernels: 40.7 us -> 41.4 us  [fused_body(): pl.pallas_call(functools.partial(kernel, (nx, ng, front, back, depth)), o...]
where the time goes in v4:
time: 46.7 us; the launch traced here: 46.4 us
  Pallas kernels  41.4 us (89%)
  local copies, waits for them, and re-layouts  3.67 us (8%)
  between operations  1.32 us (3%)
    pallas_call x1, Pallas kernels, fused_body(): pl.pallas_call(functools.partial(kernel, (nx, ng, front, back, depth)), o...  41.4 us
    unnamed x8, local copies, waits for them, and re-layouts  3.67 us

profile of v4, /device:TPU:0, one launch (start us, length us, event | category | flops | bytes accessed | tf_op | source)
XLA Modules:
  0.0 46.4 jit_solution(11943650283558557033)
XLA Ops:
  0.6 0.0 copy-start.1
  1.3 0.0 copy-done.1
  1.3 0.0 copy-start
  1.3 1.1 %copy-done = f32[48,24,128]{2,1,0:T(8,128)S(1)} copy-done((f32[48,24,128]{2,1,0:T(8,128)S(1)}, f32[48,24,128]{2,1,0:T(8,128)}, u32[]{:S(2)}) %copy-start) | copy-done | bytes 589848
  2.4 41.4 %shard_map.66 = (f32[48,64]{1,0:T(8,128)S(1)}, f32[24,64]{1,0:T(8,128)S(1)}, f32[128,64]{1,0:T(8,128)S(1)}, f32[512,128]{1,0:T(8,128)S(1)}) custom-call(s32[6]{0:T(128)S(1)} %copy-done.1, s32[1]{0:T(128)S(6)} %copy.11.top, f32[48,24,128]{2,1,0:T(8,128)S(1)} %copy-done), custom_call_target="tpu_custom_call" | custom-call | tf_op jit(solution)/shard_map/pallas_call | solution.py:492
  43.8 0.7 %copy.7 = f32[128,64]{0,1:T(8,128)} copy(f32[128,64]{1,0:T(8,128)S(1)} %get-tuple-element.14) | data formatting | bytes 65536
  44.5 0.6 %copy.12 = f32[48,64]{1,0:T(8,128)} copy(f32[48,64]{1,0:T(8,128)S(1)} %get-tuple-element.20) | data formatting | bytes 24576
  45.1 0.6 %copy.13 = f32[24,64]{1,0:T(8,128)} copy(f32[24,64]{1,0:T(8,128)S(1)} %get-tuple-element.21) | data formatting | bytes 12288
  45.7 0.7 %copy.14 = f32[32,16,128]{2,1,0:T(8,128)} copy(f32[32,16,128]{2,1,0:T(8,128)S(1)} %bitcast.1) | data formatting | bytes 524288
Async XLA Ops:
  0.6 0.7 %copy-start.1 = (s32[6]{0:T(128)S(1)}, s32[6]{0:T(128)}, u32[]{:S(2)}) copy-start(s32[6]{0:T(128)} %keys.1) | copy-start | bytes 76
  1.3 1.1 %copy-start = (f32[48,24,128]{2,1,0:T(8,128)S(1)}, f32[48,24,128]{2,1,0:T(8,128)}, u32[]{:S(2)}) copy-start(f32[48,24,128]{2,1,0:T(8,128)} %field_in.1) | copy-start | bytes 1769476
